TPU v7x, 256 devices: a whole 4x4x8 slice. The times are simulated.
256 devices in a mesh: cell: 32 (over z, y_hi, core), period: 8 (over x, y_lo).
Axes of the slice: x: 4, y: 4 (y_hi: 2, y_lo: 2; y = y_hi * 2 + y_lo), z: 8, core: 2. Of those that a mesh axis runs over, the one named last changes fastest.
Arguments:
- footprints: float32 [32, 16, 32768], P(None, 'period', 'cell'), may hold values from -16 to 16
- cell_coords: int32 [2, 32768], P(None, 'cell'), may hold values from 0 to 255, as said below
- obs_period: int32 [32], replicated, may hold values from 0 to 15
- temporal_cov: float32 [16, 16], replicated, may hold values from -1.5 to 1.5
Outputs:
- hq_field: float32 [32, 16, 32768], P(None, 'period', 'cell')
- hqh_gram: float32 [32, 32], replicated
Inputs may be any that keep to these rules, and one draw needn't show every extreme that they name: `cell_coords`: cells sit at distinct grid points that together fill the rectangle of first coordinates 0 to 255 and second coordinates 0 to 127.
All inputs are finite; a program needn't handle non-finite values.
Results may differ from a plain program's by a relative error of at most 0.0003.
Values sent between devices are 32-bit elements; how exact they have to be, the bound alone decides.
No kernel may reach another device: no remote copies, remote signals or barrier semaphores. Data moves between devices by JAX's collectives and lax.ppermute only.
A program may use at most 64 MiB of HBM per device.

v0:
```python
import jax
import jax.numpy as jnp
from jax import lax
from jax.sharding import PartitionSpec as P

LENGTH_SCALE = 48.0
BLOCK_LIMIT = 4096


def covariance_tile(first_xy, second_xy):
    delta_x = first_xy[0][:, None] - second_xy[0][None, :]
    delta_y = first_xy[1][:, None] - second_xy[1][None, :]
    return jnp.exp(-jnp.sqrt(delta_x * delta_x + delta_y * delta_y) / LENGTH_SCALE)


def block_size(total_width, unit_width):
    unit_count = total_width // unit_width
    best_count = 1
    for factor in range(1, unit_count + 1):
        if unit_count % factor == 0 and factor * unit_width <= max(BLOCK_LIMIT, unit_width):
            best_count = factor
    return best_count * unit_width


def on_device(footprints, cell_coords, obs_period, temporal_cov):
    obs_count, per_local, cell_local = footprints.shape
    flat_count = obs_count * per_local
    period_first = lax.axis_index("period") * per_local
    period_ids = period_first + jnp.arange(per_local, dtype=jnp.int32)
    keep = (period_ids[None, :, None] <= obs_period[:, None, None]).astype(jnp.float32)
    masked = footprints * keep
    flat_rows = masked.reshape(flat_count, cell_local)
    local_places = cell_coords.astype(jnp.float32)
    empty = jnp.zeros((flat_count, cell_local), jnp.float32)
    piece_rows = lax.all_gather(flat_rows, "cell", axis=1, tiled=True)
    piece_places = lax.all_gather(local_places, "cell", axis=1, tiled=True)
    piece_width = piece_rows.shape[1]
    block_width = block_size(piece_width, cell_local)

    def add_block(block_index, running_sum):
        offset = block_index * block_width
        part_rows = lax.dynamic_slice_in_dim(piece_rows, offset, block_width, 1)
        part_places = lax.dynamic_slice_in_dim(piece_places, offset, block_width, 1)
        tile = covariance_tile(part_places, local_places)
        return running_sum + jnp.dot(
            part_rows, tile, precision=lax.Precision.HIGHEST, preferred_element_type=jnp.float32
        )

    spatial_flat = lax.fori_loop(0, piece_width // block_width, add_block, empty)
    spatial = spatial_flat.reshape(obs_count, per_local, cell_local)
    piece = lax.all_gather(spatial, "period", axis=1, tiled=True)
    weights = lax.dynamic_slice(temporal_cov, (period_first, 0), (per_local, piece.shape[1]))
    hq_field = jnp.einsum("tu,nuj->ntj", weights, piece, precision=lax.Precision.HIGHEST)
    partial_gram = jnp.einsum("ntj,mtj->nm", hq_field, masked, precision=lax.Precision.HIGHEST)
    hqh_gram = lax.psum(partial_gram, ("cell", "period"))
    return (hq_field, hqh_gram)


def solution(mesh):
    return jax.shard_map(
        on_device,
        mesh=mesh,
        in_specs=(P(None, "period", "cell"), P(None, "cell"), P(), P()),
        out_specs=(P(None, "period", "cell"), P()),
        check_vma=False,
    )
```

profile of v0, /device:TPU:1, one launch (start us, length us, event | category | flops | bytes accessed | tf_op | source)
XLA Modules:
  0.0 412.7 jit_solution(13719887616135554057)
XLA Ops:
  7.2 0.0 copy-start
  7.2 0.0 all-gather.3.cloned.1.call-start
  7.2 0.7 compare_convert_fusion
  8.0 0.1 copy.15
  8.1 1.1 broadcast_multiply_fusion
  9.2 0.9 reshape.51
  10.0 0.0 all-gather.3.cloned.1.call-update
  10.1 0.0 all-gather.5.cloned.1.call-start
  10.1 0.7 convert_element_type.12
  10.8 47.3 %all_gather.10 = f32[2,32768]{1,0:T(2,128)S(1)} all-gather(f32[2,1024]{1,0:T(2,128)S(1)} %convert_element_type.12), channel_id=1, replica_groups=mesh['cell'=32,'period'=8] {'cell'}, dimensions={1}, use_global_device_ids=true | all-gather | bytes 270336 | tf_op jit(solution)/shard_map/all_gather | solution.py:36
  58.1 58.6 %all-gather.3.cloned.1.call-done = f32[64,32768]{1,0:T(8,128)} async-done(((f32[64,1024]{1,0:T(8,128)}), f32[64,32768]{1,0:T(8,128)}) %all-gather.3.cloned.1.call-update) | async-done | bytes 8388624 | tf_op jit(solution)/shard_map/all_gather | solution.py:35
  116.7 157.3 %while.14 = (s32[]{:T(128)}, f32[64,1024]{1,0:T(8,128)S(1)}, f32[64,32768]{1,0:T(8,128)}, f32[2,32768]{1,0:T(2,128)S(1)}, f32[2,1024]{1,0:T(2,128)S(1)}, /*index...) while((s32[]{:T(128)}, f32[64,1024]{1,0:T(8,128)S(1)}, f32[64,32768]{1,0:T(8,128)}, ...), condition=%wide.region_1.0_spmd.clone, body=%wide.region_0.0_spmd.clone.sunk | while | flops 3250716672 | bytes 1695933 | solution.py:49
  116.7 0.1 constant_dynamic-slice_fusion.2
  116.8 19.5 %fusion.39 = f32[64,1024]{1,0:T(8,128)S(1)} fusion(f32[1024]{0:T(1024)S(1)} %bitcast.22, f32[4096]{0:T(1024)S(1)} %bitcast.20, f32[1024]{0:T(1024)S(1)} %bitcast.21, f32[4096]{0:T(1024)S(1)} %bitcast.19, f32[64,32768]{1,0:T(8,128)} %get-tuple-element.190, s32[]{:T(128)S(6)} %select_n.14, f32[64,1024]{1,0:T(8,128)S(1)} %get-tuple-element.179, ...), kind=kOutput, calls=%fused_computation.15.clone.1 | convolution fusion | flops 3250716672 | bytes 1613829 | tf_op jit(solution)/shard_map/while/body/eval_jaxpr/dot_general | solution.py:45
  136.3 0.1 constant_dynamic-slice_fusion.2
  136.4 19.5 %fusion.39 = f32[64,1024]{1,0:T(8,128)S(1)} fusion(f32[1024]{0:T(1024)S(1)} %bitcast.22, f32[4096]{0:T(1024)S(1)} %bitcast.20, f32[1024]{0:T(1024)S(1)} %bitcast.21, f32[4096]{0:T(1024)S(1)} %bitcast.19, f32[64,32768]{1,0:T(8,128)} %get-tuple-element.190, s32[]{:T(128)S(6)} %select_n.14, f32[64,1024]{1,0:T(8,128)S(1)} %get-tuple-element.179, ...), kind=kOutput, calls=%fused_computation.15.clone.1 | convolution fusion | flops 3250716672 | bytes 1613829 | tf_op jit(solution)/shard_map/while/body/eval_jaxpr/dot_general | solution.py:45
  156.0 0.1 constant_dynamic-slice_fusion.2
  156.1 19.5 %fusion.39 = f32[64,1024]{1,0:T(8,128)S(1)} fusion(f32[1024]{0:T(1024)S(1)} %bitcast.22, f32[4096]{0:T(1024)S(1)} %bitcast.20, f32[1024]{0:T(1024)S(1)} %bitcast.21, f32[4096]{0:T(1024)S(1)} %bitcast.19, f32[64,32768]{1,0:T(8,128)} %get-tuple-element.190, s32[]{:T(128)S(6)} %select_n.14, f32[64,1024]{1,0:T(8,128)S(1)} %get-tuple-element.179, ...), kind=kOutput, calls=%fused_computation.15.clone.1 | convolution fusion | flops 3250716672 | bytes 1613829 | tf_op jit(solution)/shard_map/while/body/eval_jaxpr/dot_general | solution.py:45
  175.6 0.1 constant_dynamic-slice_fusion.2
  175.7 19.5 %fusion.39 = f32[64,1024]{1,0:T(8,128)S(1)} fusion(f32[1024]{0:T(1024)S(1)} %bitcast.22, f32[4096]{0:T(1024)S(1)} %bitcast.20, f32[1024]{0:T(1024)S(1)} %bitcast.21, f32[4096]{0:T(1024)S(1)} %bitcast.19, f32[64,32768]{1,0:T(8,128)} %get-tuple-element.190, s32[]{:T(128)S(6)} %select_n.14, f32[64,1024]{1,0:T(8,128)S(1)} %get-tuple-element.179, ...), kind=kOutput, calls=%fused_computation.15.clone.1 | convolution fusion | flops 3250716672 | bytes 1613829 | tf_op jit(solution)/shard_map/while/body/eval_jaxpr/dot_general | solution.py:45
  195.3 0.1 constant_dynamic-slice_fusion.2
  195.4 19.5 %fusion.39 = f32[64,1024]{1,0:T(8,128)S(1)} fusion(f32[1024]{0:T(1024)S(1)} %bitcast.22, f32[4096]{0:T(1024)S(1)} %bitcast.20, f32[1024]{0:T(1024)S(1)} %bitcast.21, f32[4096]{0:T(1024)S(1)} %bitcast.19, f32[64,32768]{1,0:T(8,128)} %get-tuple-element.190, s32[]{:T(128)S(6)} %select_n.14, f32[64,1024]{1,0:T(8,128)S(1)} %get-tuple-element.179, ...), kind=kOutput, calls=%fused_computation.15.clone.1 | convolution fusion | flops 3250716672 | bytes 1613829 | tf_op jit(solution)/shard_map/while/body/eval_jaxpr/dot_general | solution.py:45
  214.9 0.1 constant_dynamic-slice_fusion.2
  215.0 19.5 %fusion.39 = f32[64,1024]{1,0:T(8,128)S(1)} fusion(f32[1024]{0:T(1024)S(1)} %bitcast.22, f32[4096]{0:T(1024)S(1)} %bitcast.20, f32[1024]{0:T(1024)S(1)} %bitcast.21, f32[4096]{0:T(1024)S(1)} %bitcast.19, f32[64,32768]{1,0:T(8,128)} %get-tuple-element.190, s32[]{:T(128)S(6)} %select_n.14, f32[64,1024]{1,0:T(8,128)S(1)} %get-tuple-element.179, ...), kind=kOutput, calls=%fused_computation.15.clone.1 | convolution fusion | flops 3250716672 | bytes 1613829 | tf_op jit(solution)/shard_map/while/body/eval_jaxpr/dot_general | solution.py:45
  234.6 0.1 constant_dynamic-slice_fusion.2
  234.7 19.5 %fusion.39 = f32[64,1024]{1,0:T(8,128)S(1)} fusion(f32[1024]{0:T(1024)S(1)} %bitcast.22, f32[4096]{0:T(1024)S(1)} %bitcast.20, f32[1024]{0:T(1024)S(1)} %bitcast.21, f32[4096]{0:T(1024)S(1)} %bitcast.19, f32[64,32768]{1,0:T(8,128)} %get-tuple-element.190, s32[]{:T(128)S(6)} %select_n.14, f32[64,1024]{1,0:T(8,128)S(1)} %get-tuple-element.179, ...), kind=kOutput, calls=%fused_computation.15.clone.1 | convolution fusion | flops 3250716672 | bytes 1613829 | tf_op jit(solution)/shard_map/while/body/eval_jaxpr/dot_general | solution.py:45
  254.2 0.1 constant_dynamic-slice_fusion.2
  254.3 19.5 %fusion.39 = f32[64,1024]{1,0:T(8,128)S(1)} fusion(f32[1024]{0:T(1024)S(1)} %bitcast.22, f32[4096]{0:T(1024)S(1)} %bitcast.20, f32[1024]{0:T(1024)S(1)} %bitcast.21, f32[4096]{0:T(1024)S(1)} %bitcast.19, f32[64,32768]{1,0:T(8,128)} %get-tuple-element.190, s32[]{:T(128)S(6)} %select_n.14, f32[64,1024]{1,0:T(8,128)S(1)} %get-tuple-element.179, ...), kind=kOutput, calls=%fused_computation.15.clone.1 | convolution fusion | flops 3250716672 | bytes 1613829 | tf_op jit(solution)/shard_map/while/body/eval_jaxpr/dot_general | solution.py:45
  274.0 0.1 reshape.52
  274.2 0.8 copy.16
  275.0 0.0 all-gather.5.cloned.1.call-update
  275.0 48.4 %all-gather.5.cloned.1.call-done = f32[32,16,1024]{2,0,1:T(8,128)} async-done(((f32[32,2,1024]{2,0,1:T(8,128)}), f32[32,16,1024]{2,0,1:T(8,128)}) %all-gather.5.cloned.1.call-update) | async-done | bytes 2097168 | tf_op jit(solution)/shard_map/all_gather | solution.py:51
  323.4 0.0 copy-done
  323.4 3.9 fusion.23
  327.3 0.0 copy-start.1
  327.3 0.5 convolution_bitcast_fusion
  327.7 78.1 %psum.7 = f32[32,32]{1,0:T(8,128)} all-reduce(f32[32,32]{1,0:T(8,128)S(1)} %convolution_bitcast_fusion), channel_id=1, replica_groups=mesh['cell'=32,'period'=8] {'cell','period'}, use_global_device_ids=true, to_apply=%region_2.0 | all-reduce | flops 1024 | bytes 8192 | tf_op jit(solution)/shard_map/psum | solution.py:55
  405.8 0.0 copy-done.1
  (10 shorter events, 0.1 us)
Async XLA Ops:
  7.2 316.2 %copy-start = (f32[16,16]{1,0:T(8,128)S(1)}, f32[16,16]{1,0:T(8,128)}, u32[]{:S(2)}) copy-start(f32[16,16]{1,0:T(8,128)} %param.9) | copy-start | bytes 3076
  7.2 109.5 %all-gather.3.cloned.1.call-start = ((), (), s32[]{:S(2)}) async-start(), calls=%async_computation | async-start | bytes 8650752 | tf_op jit(solution)/shard_map/all_gather | solution.py:35
  10.1 313.3 %all-gather.5.cloned.1.call-start = ((), (), s32[]{:S(2)}) async-start(), calls=%async_computation.1 | async-start | bytes 2359296 | tf_op jit(solution)/shard_map/all_gather | solution.py:51
  327.3 78.6 %copy-start.1 = (f32[32,2,1024]{2,1,0:T(2,128)}, f32[32,2,1024]{2,1,0:T(2,128)S(1)}, u32[]{:S(2)}) copy-start(f32[32,2,1024]{2,1,0:T(2,128)S(1)} %fusion.23) | copy-start | bytes 786436
Sparse Core Ops, SparseCore 0:
  11.4 105.2 all-gather.2
  275.1 48.2 all-gather.4
where the time goes:
time: 413 us
  matrix products  160 us (39%)
  blocking collectives  125 us (30%)
  waiting for transfers between devices  107 us (26%)
  between operations  14.1 us (3%)
    dot_general x8, matrix products, add_block(): jnp.dot(part_rows, tile, precision=lax.Precision.HIGHEST, preferred_eleme...  156 us
    psum x1, blocking collectives, on_device(): hqh_gram = lax.psum(partial_gram, ('cell', 'period'))  78.1 us
    all_gather x1, waiting for transfers between devices, on_device(): piece_rows = lax.all_gather(flat_rows, 'cell', axis=1, tiled=True)  58.6 us
    all_gather x1, waiting for transfers between devices, on_device(): piece = lax.all_gather(spatial, 'period', axis=1, tiled=True)  48.4 us
    all_gather x1, blocking collectives, on_device(): piece_places = lax.all_gather(local_places, 'cell', axis=1, tiled=True)  47.3 us
  transfers between devices with their start and end apart: 2, of which 2 were waited for; matrix products, arithmetic and copies ran while one was open for 0% of the time, Pallas kernels for 0%

commit v1 on v0

--- a/solution.py
+++ b/solution.py
@@ -52,7 +52,7 @@
     weights = lax.dynamic_slice(temporal_cov, (period_first, 0), (per_local, piece.shape[1]))
     hq_field = jnp.einsum("tu,nuj->ntj", weights, piece, precision=lax.Precision.HIGHEST)
     partial_gram = jnp.einsum("ntj,mtj->nm", hq_field, masked, precision=lax.Precision.HIGHEST)
-    hqh_gram = lax.psum(partial_gram, ("cell", "period"))
+    hqh_gram = lax.psum(lax.psum(partial_gram, "period"), "cell")
     return (hq_field, hqh_gram)
 
 

time: 413 us -> 496 us (1.20)
  blocking collectives: 125 us -> 205 us
    psum x1 -> x2, blocking collectives: 78.1 us -> 158 us  [on_device(): hqh_gram = lax.psum(lax.psum(partial_gram, 'period'), 'cell')]
where the time goes in v1:
time: 496 us; the launch traced here: 492 us
  blocking collectives  205 us (41%)
  matrix products  160 us (32%)
  waiting for transfers between devices  107 us (22%)
  between operations  14.1 us (3%)
    psum x2, blocking collectives, on_device(): hqh_gram = lax.psum(lax.psum(partial_gram, 'period'), 'cell')  158 us
    dot_general x8, matrix products, add_block(): jnp.dot(part_rows, tile, precision=lax.Precision.HIGHEST, preferred_eleme...  156 us
    all_gather x1, waiting for transfers between devices, on_device(): piece_rows = lax.all_gather(flat_rows, 'cell', axis=1, tiled=True)  58.6 us
    all_gather x1, waiting for transfers between devices, on_device(): piece = lax.all_gather(spatial, 'period', axis=1, tiled=True)  48.4 us
    all_gather x1, blocking collectives, on_device(): piece_places = lax.all_gather(local_places, 'cell', axis=1, tiled=True)  47.3 us
  transfers between devices with their start and end apart: 2, of which 2 were waited for; matrix products, arithmetic and copies ran while one was open for 0% of the time, Pallas kernels for 0%

profile of v1, /device:TPU:1, one launch (start us, length us, event | category | flops | bytes accessed | tf_op | source)
XLA Modules:
  0.0 492.4 jit_solution(5073723794767255577)
XLA Ops:
  7.2 0.0 copy-start
  7.2 0.0 all-gather.3.cloned.1.call-start
  7.2 0.7 compare_convert_fusion
  8.0 0.1 copy.15
  8.1 1.1 broadcast_multiply_fusion
  9.2 0.9 reshape.51
  10.0 0.0 all-gather.3.cloned.1.call-update
  10.1 0.0 all-gather.5.cloned.1.call-start
  10.1 0.7 convert_element_type.12
  10.8 47.3 %all_gather.10 = f32[2,32768]{1,0:T(2,128)S(1)} all-gather(f32[2,1024]{1,0:T(2,128)S(1)} %convert_element_type.12), channel_id=1, replica_groups=mesh['cell'=32,'period'=8] {'cell'}, dimensions={1}, use_global_device_ids=true | all-gather | bytes 270336 | tf_op jit(solution)/shard_map/all_gather | solution.py:36
  58.1 58.6 %all-gather.3.cloned.1.call-done = f32[64,32768]{1,0:T(8,128)} async-done(((f32[64,1024]{1,0:T(8,128)}), f32[64,32768]{1,0:T(8,128)}) %all-gather.3.cloned.1.call-update) | async-done | bytes 8388624 | tf_op jit(solution)/shard_map/all_gather | solution.py:35
  116.7 157.3 %while.14 = (s32[]{:T(128)}, f32[64,1024]{1,0:T(8,128)S(1)}, f32[64,32768]{1,0:T(8,128)}, f32[2,32768]{1,0:T(2,128)S(1)}, f32[2,1024]{1,0:T(2,128)S(1)}, /*index...) while((s32[]{:T(128)}, f32[64,1024]{1,0:T(8,128)S(1)}, f32[64,32768]{1,0:T(8,128)}, ...), condition=%wide.region_1.0_spmd.clone, body=%wide.region_0.0_spmd.clone.sunk | while | flops 3250716672 | bytes 1695933 | solution.py:49
  116.7 0.1 constant_dynamic-slice_fusion.2
  116.8 19.5 %fusion.39 = f32[64,1024]{1,0:T(8,128)S(1)} fusion(f32[1024]{0:T(1024)S(1)} %bitcast.22, f32[4096]{0:T(1024)S(1)} %bitcast.20, f32[1024]{0:T(1024)S(1)} %bitcast.21, f32[4096]{0:T(1024)S(1)} %bitcast.19, f32[64,32768]{1,0:T(8,128)} %get-tuple-element.190, s32[]{:T(128)S(6)} %select_n.14, f32[64,1024]{1,0:T(8,128)S(1)} %get-tuple-element.179, ...), kind=kOutput, calls=%fused_computation.15.clone.1 | convolution fusion | flops 3250716672 | bytes 1613829 | tf_op jit(solution)/shard_map/while/body/eval_jaxpr/dot_general | solution.py:45
  136.3 0.1 constant_dynamic-slice_fusion.2
  136.4 19.5 %fusion.39 = f32[64,1024]{1,0:T(8,128)S(1)} fusion(f32[1024]{0:T(1024)S(1)} %bitcast.22, f32[4096]{0:T(1024)S(1)} %bitcast.20, f32[1024]{0:T(1024)S(1)} %bitcast.21, f32[4096]{0:T(1024)S(1)} %bitcast.19, f32[64,32768]{1,0:T(8,128)} %get-tuple-element.190, s32[]{:T(128)S(6)} %select_n.14, f32[64,1024]{1,0:T(8,128)S(1)} %get-tuple-element.179, ...), kind=kOutput, calls=%fused_computation.15.clone.1 | convolution fusion | flops 3250716672 | bytes 1613829 | tf_op jit(solution)/shard_map/while/body/eval_jaxpr/dot_general | solution.py:45
  156.0 0.1 constant_dynamic-slice_fusion.2
  156.1 19.5 %fusion.39 = f32[64,1024]{1,0:T(8,128)S(1)} fusion(f32[1024]{0:T(1024)S(1)} %bitcast.22, f32[4096]{0:T(1024)S(1)} %bitcast.20, f32[1024]{0:T(1024)S(1)} %bitcast.21, f32[4096]{0:T(1024)S(1)} %bitcast.19, f32[64,32768]{1,0:T(8,128)} %get-tuple-element.190, s32[]{:T(128)S(6)} %select_n.14, f32[64,1024]{1,0:T(8,128)S(1)} %get-tuple-element.179, ...), kind=kOutput, calls=%fused_computation.15.clone.1 | convolution fusion | flops 3250716672 | bytes 1613829 | tf_op jit(solution)/shard_map/while/body/eval_jaxpr/dot_general | solution.py:45
  175.6 0.1 constant_dynamic-slice_fusion.2
  175.7 19.5 %fusion.39 = f32[64,1024]{1,0:T(8,128)S(1)} fusion(f32[1024]{0:T(1024)S(1)} %bitcast.22, f32[4096]{0:T(1024)S(1)} %bitcast.20, f32[1024]{0:T(1024)S(1)} %bitcast.21, f32[4096]{0:T(1024)S(1)} %bitcast.19, f32[64,32768]{1,0:T(8,128)} %get-tuple-element.190, s32[]{:T(128)S(6)} %select_n.14, f32[64,1024]{1,0:T(8,128)S(1)} %get-tuple-element.179, ...), kind=kOutput, calls=%fused_computation.15.clone.1 | convolution fusion | flops 3250716672 | bytes 1613829 | tf_op jit(solution)/shard_map/while/body/eval_jaxpr/dot_general | solution.py:45
  195.3 0.1 constant_dynamic-slice_fusion.2
  195.4 19.5 %fusion.39 = f32[64,1024]{1,0:T(8,128)S(1)} fusion(f32[1024]{0:T(1024)S(1)} %bitcast.22, f32[4096]{0:T(1024)S(1)} %bitcast.20, f32[1024]{0:T(1024)S(1)} %bitcast.21, f32[4096]{0:T(1024)S(1)} %bitcast.19, f32[64,32768]{1,0:T(8,128)} %get-tuple-element.190, s32[]{:T(128)S(6)} %select_n.14, f32[64,1024]{1,0:T(8,128)S(1)} %get-tuple-element.179, ...), kind=kOutput, calls=%fused_computation.15.clone.1 | convolution fusion | flops 3250716672 | bytes 1613829 | tf_op jit(solution)/shard_map/while/body/eval_jaxpr/dot_general | solution.py:45
  214.9 0.1 constant_dynamic-slice_fusion.2
  215.0 19.5 %fusion.39 = f32[64,1024]{1,0:T(8,128)S(1)} fusion(f32[1024]{0:T(1024)S(1)} %bitcast.22, f32[4096]{0:T(1024)S(1)} %bitcast.20, f32[1024]{0:T(1024)S(1)} %bitcast.21, f32[4096]{0:T(1024)S(1)} %bitcast.19, f32[64,32768]{1,0:T(8,128)} %get-tuple-element.190, s32[]{:T(128)S(6)} %select_n.14, f32[64,1024]{1,0:T(8,128)S(1)} %get-tuple-element.179, ...), kind=kOutput, calls=%fused_computation.15.clone.1 | convolution fusion | flops 3250716672 | bytes 1613829 | tf_op jit(solution)/shard_map/while/body/eval_jaxpr/dot_general | solution.py:45
  234.6 0.1 constant_dynamic-slice_fusion.2
  234.7 19.5 %fusion.39 = f32[64,1024]{1,0:T(8,128)S(1)} fusion(f32[1024]{0:T(1024)S(1)} %bitcast.22, f32[4096]{0:T(1024)S(1)} %bitcast.20, f32[1024]{0:T(1024)S(1)} %bitcast.21, f32[4096]{0:T(1024)S(1)} %bitcast.19, f32[64,32768]{1,0:T(8,128)} %get-tuple-element.190, s32[]{:T(128)S(6)} %select_n.14, f32[64,1024]{1,0:T(8,128)S(1)} %get-tuple-element.179, ...), kind=kOutput, calls=%fused_computation.15.clone.1 | convolution fusion | flops 3250716672 | bytes 1613829 | tf_op jit(solution)/shard_map/while/body/eval_jaxpr/dot_general | solution.py:45
  254.2 0.1 constant_dynamic-slice_fusion.2
  254.3 19.5 %fusion.39 = f32[64,1024]{1,0:T(8,128)S(1)} fusion(f32[1024]{0:T(1024)S(1)} %bitcast.22, f32[4096]{0:T(1024)S(1)} %bitcast.20, f32[1024]{0:T(1024)S(1)} %bitcast.21, f32[4096]{0:T(1024)S(1)} %bitcast.19, f32[64,32768]{1,0:T(8,128)} %get-tuple-element.190, s32[]{:T(128)S(6)} %select_n.14, f32[64,1024]{1,0:T(8,128)S(1)} %get-tuple-element.179, ...), kind=kOutput, calls=%fused_computation.15.clone.1 | convolution fusion | flops 3250716672 | bytes 1613829 | tf_op jit(solution)/shard_map/while/body/eval_jaxpr/dot_general | solution.py:45
  274.0 0.1 reshape.52
  274.2 0.8 copy.16
  275.0 0.0 all-gather.5.cloned.1.call-update
  275.0 48.4 %all-gather.5.cloned.1.call-done = f32[32,16,1024]{2,0,1:T(8,128)} async-done(((f32[32,2,1024]{2,0,1:T(8,128)}), f32[32,16,1024]{2,0,1:T(8,128)}) %all-gather.5.cloned.1.call-update) | async-done | bytes 2097168 | tf_op jit(solution)/shard_map/all_gather | solution.py:51
  323.4 0.0 copy-done
  323.4 3.9 fusion.23
  327.3 0.0 copy-start.1
  327.3 0.5 convolution_bitcast_fusion
  327.7 26.5 %psum.14 = f32[32,32]{1,0:T(8,128)S(1)} all-reduce(f32[32,32]{1,0:T(8,128)S(1)} %convolution_bitcast_fusion), channel_id=1, replica_groups=mesh['cell'=32,'period'=8] {'period'}, use_global_device_ids=true, to_apply=%region_2.0 | all-reduce | flops 1024 | bytes 8192 | tf_op jit(solution)/shard_map/psum | solution.py:55
  354.2 131.3 %psum.15 = f32[32,32]{1,0:T(8,128)} all-reduce(f32[32,32]{1,0:T(8,128)S(1)} %psum.14), channel_id=1, replica_groups=mesh['cell'=32,'period'=8] {'cell'}, use_global_device_ids=true, to_apply=%region_3.0 | all-reduce | flops 1024 | bytes 8192 | tf_op jit(solution)/shard_map/psum | solution.py:55
  485.5 0.0 copy-done.1
  (10 shorter events, 0.1 us)
Async XLA Ops:
  7.2 316.2 %copy-start = (f32[16,16]{1,0:T(8,128)S(1)}, f32[16,16]{1,0:T(8,128)}, u32[]{:S(2)}) copy-start(f32[16,16]{1,0:T(8,128)} %param.9) | copy-start | bytes 3076
  7.2 109.5 %all-gather.3.cloned.1.call-start = ((), (), s32[]{:S(2)}) async-start(), calls=%async_computation | async-start | bytes 8650752 | tf_op jit(solution)/shard_map/all_gather | solution.py:35
  10.1 313.3 %all-gather.5.cloned.1.call-start = ((), (), s32[]{:S(2)}) async-start(), calls=%async_computation.1 | async-start | bytes 2359296 | tf_op jit(solution)/shard_map/all_gather | solution.py:51
  327.3 158.3 %copy-start.1 = (f32[32,2,1024]{2,1,0:T(2,128)}, f32[32,2,1024]{2,1,0:T(2,128)S(1)}, u32[]{:S(2)}) copy-start(f32[32,2,1024]{2,1,0:T(2,128)S(1)} %fusion.23) | copy-start | bytes 786436
Sparse Core Ops, SparseCore 0:
  11.4 105.2 all-gather.2
  275.1 48.2 all-gather.4
